TPU v7x, 128 devices: a whole 4x4x4 slice. The times are simulated.
128 devices in a mesh: row: 8 (over x, core), col: 16 (over y, z).
Axes of the slice: x: 4, y: 4, z: 4, core: 2. Of those that a mesh axis runs over, the one named last changes fastest.
Arguments:
- parent_front: float32 [16384, 16384], P('row', 'col'), as said below
- child_panels: float32 [8, 4096, 512], P('row', 'col'), may hold values from -6 to 6
- child_inverses: float32 [8, 512, 512], P('row'), as said below
- parent_index: int32 [8, 16], replicated, may hold values from 2 to 63, as said below
Outputs:
- panel: float32 [16384, 512], P('row')
- schur: float32 [16384, 16384], P('row', 'col')
Inputs may be any that keep to these rules, and one draw needn't show every extreme that they name: `parent_index`: entry (g, u) names the parent tile that receives tile row and tile column u of child g's update. Seen in blocks of 4 consecutive tiles, each child names every block exactly once, and at a given u the children name different blocks. No entry names one of the first 2 tiles. `parent_front`: Symmetric. In its leading 2 * 256 rows and columns, each diagonal entry is positive and exceeds the sum of magnitudes of the other entries of its row within that block. `child_inverses`: each matrix is lower triangular with a positive diagonal.
All inputs are finite; a program needn't handle non-finite values.
Results may differ from a plain program's by a relative error of at most 0.0003.
Values sent between devices are 32-bit elements; how exact they have to be, the bound alone decides.
A program may use at most 128 MiB of HBM per device.

v0:
```python
import jax
import jax.numpy as jnp
from jax import lax
from jax.sharding import PartitionSpec as P

TILE = 256
PCT = 4
NSP = 2


def from_root(block, axis, holder):
    block = jnp.where(lax.axis_index(axis) == holder, block, jnp.zeros_like(block))
    return lax.psum(block, axis)


def product(matrix_a, matrix_b):
    return jnp.dot(
        matrix_a, matrix_b, precision=lax.Precision.HIGHEST, preferred_element_type=jnp.float32
    )


def product_rows(matrix_a, matrix_b):
    return lax.dot_general(
        matrix_a,
        matrix_b,
        (((1,), (1,)), ((), ())),
        precision=lax.Precision.HIGHEST,
        preferred_element_type=jnp.float32,
    )


def place_tiles(received, row_tiles, col_tiles, live_mask, tile_count):
    target = row_tiles * PCT + col_tiles
    onehot = (target[None, :] == jnp.arange(tile_count)[:, None]).astype(jnp.float32) * live_mask[
        None, :
    ]
    flat_tiles = received.reshape(received.shape[0], TILE * TILE)
    return product(onehot, flat_tiles)


def per_device(parent_front, child_panels, child_inverses, parent_index):
    row_devices = lax.axis_size("row")
    col_devices = lax.axis_size("col")
    here_row = lax.axis_index("row")
    here_col = lax.axis_index("col")
    per_block = col_devices // row_devices
    row_count = PCT * per_block
    tile_count = row_count * PCT
    own_factor = product_rows(child_panels[0], child_inverses[0])
    my_list = lax.dynamic_index_in_dim(parent_index, here_row, 0, keepdims=False)
    block_of = parent_index // PCT
    update_col = product_rows(lax.all_gather(own_factor, "col", axis=0, tiled=True), own_factor)
    dest_row = my_list // PCT // per_block
    tile_ids = jnp.arange(col_devices, dtype=jnp.int32)
    same_dest = (dest_row[None, :] == dest_row[:, None]) & (tile_ids[None, :] < tile_ids[:, None])
    slot_index = jnp.sum(same_dest.astype(jnp.int32), axis=1)
    position = dest_row * per_block + slot_index
    send_order = jnp.zeros((col_devices,), jnp.int32).at[position].set(tile_ids)
    outgoing = update_col.reshape(col_devices, TILE, TILE)[send_order].reshape(
        row_devices, per_block, TILE, TILE
    )
    arrived = lax.all_to_all(outgoing, "row", split_axis=0, concat_axis=0, tiled=True)
    local_mask = block_of // per_block == here_row
    slot_rank = jnp.cumsum(local_mask.astype(jnp.int32), axis=1) - 1
    slot_ids = jnp.arange(per_block, dtype=jnp.int32)
    slot_pick = (
        local_mask[:, :, None] & (slot_rank[:, :, None] == slot_ids[None, None, :])
    ).astype(jnp.int32)
    row_tile = jnp.sum(parent_index[:, :, None] * slot_pick, axis=1) - here_row * row_count
    sent_to = lax.dynamic_index_in_dim(block_of, here_col, 1, keepdims=False)
    col_route = (sent_to[None, :] == jnp.arange(col_devices)[:, None]).astype(jnp.float32)
    outgoing_cols = product(col_route, arrived.reshape(row_devices, -1)).reshape(
        col_devices, per_block, TILE, TILE
    )
    arrived_cols = lax.all_to_all(outgoing_cols, "col", split_axis=0, concat_axis=0, tiled=True)
    col_match = (block_of == here_col).astype(jnp.int32)
    col_tile = parent_index - here_col * PCT
    rows_from = jnp.sum(row_tile[:, None, :] * col_match[:, :, None], axis=0)
    cols_from = jnp.sum(col_tile * col_match, axis=0)
    live_from = jnp.sum(col_match, axis=0).astype(jnp.float32)
    cols_flat = (cols_from[:, None] + jnp.zeros_like(rows_from)).reshape(-1)
    live_flat = (live_from[:, None] + jnp.zeros(rows_from.shape, jnp.float32)).reshape(-1)
    contrib = place_tiles(
        arrived_cols.reshape(-1, TILE, TILE),
        rows_from.reshape(-1),
        cols_flat,
        live_flat,
        tile_count,
    )
    contrib = (
        contrib.reshape(row_count, PCT, TILE, TILE)
        .transpose(0, 2, 1, 3)
        .reshape(row_count * TILE, PCT * TILE)
    )
    work_matrix = parent_front - contrib
    identity = jnp.eye(TILE, dtype=jnp.float32)
    owner = (here_row == 0) & (here_col == 0)
    row_tile_index = here_row * row_count + jnp.arange(row_count * TILE) // TILE
    columns = []
    for step in range(NSP):
        offset = step * TILE
        diag_tile = jnp.where(
            owner, work_matrix[offset : offset + TILE, offset : offset + TILE], identity
        )
        pivot_tile = jnp.linalg.cholesky(diag_tile)
        inverse = lax.linalg.triangular_solve(pivot_tile, identity, left_side=True, lower=True)
        pivot_pair = from_root(jnp.stack([pivot_tile, inverse]), "row", 0)
        pivot_tile = pivot_pair[0]
        inverse = pivot_pair[1]
        factored = product_rows(work_matrix[:, offset : offset + TILE], inverse)
        factored = jnp.where(row_tile_index[:, None] < step, jnp.zeros_like(factored), factored)
        current = factored[offset : offset + TILE]
        rows_panel, inverse = (
            from_root(
                factored.at[offset : offset + TILE].set(
                    jnp.where(here_row == 0, pivot_tile, current)
                ),
                "col",
                0,
            ),
            from_root(inverse, "col", 0),
        )
        source = from_root(rows_panel, "row", here_col // per_block)
        col_panel = lax.dynamic_slice_in_dim(
            source, here_col % per_block * PCT * TILE, PCT * TILE, 0
        )
        work_matrix = work_matrix - product_rows(rows_panel, col_panel)
        columns.append(rows_panel)
    return (jnp.concatenate(columns, axis=1), work_matrix)


def solution(mesh):
    placed = (P("row", "col"), P("row", "col", None), P("row", None, None), P())
    return jax.shard_map(
        per_device,
        mesh=mesh,
        in_specs=placed,
        out_specs=(P("row", None), P("row", "col")),
        check_vma=False,
    )
```

profile of v0, /device:TPU:0, one launch (start us, length us, event | category | flops | bytes accessed | tf_op | source)
XLA Modules:
  0.0 993.7 jit_solution(9929762409883196764)
XLA Ops:
  7.2 1.2 copy-done
  8.4 2.9 fusion.5
  11.3 0.7 and_select_fusion
  12.0 0.7 fusion.60
  12.9 0.7 fusion.59
  13.6 0.6 scatter_custom_fusion
  14.3 70.5 %all-gather.2.cloned.1.call-done = f32[4096,512]{1,0:T(8,128)} async-done(((f32[256,512]{1,0:T(8,128)}), f32[4096,512]{1,0:T(8,128)}) %all-gather.2.cloned.1.call-update) | async-done | bytes 8388624 | tf_op jit(solution)/shard_map/all_gather | solution.py:52
  84.8 10.6 %fusion.69 = f32[4096,256]{1,0:T(8,128)} fusion(f32[4096,512]{1,0:T(8,128)} %all-gather.2.cloned.1.call-done, f32[256,512]{1,0:T(8,128)} %fusion.5), kind=kOutput, calls=%fused_computation.186 | convolution fusion | flops 6442450944 | bytes 13107200 | tf_op jit(solution)/shard_map/dot_general | solution.py:23
  95.4 5.0 gather_fusion
  100.4 4.8 all-to-all-start
  105.5 49.4 %all-to-all-done = f32[8,2,256,256]{3,2,1,0:T(8,128)} async-done(((f32[8,2,256,256]{3,2,1,0:T(8,128)}), f32[8,2,256,256]{3,2,1,0:T(8,128)}, u32[]{:S(2)}, u32[]{:S(2)}) %all-to-all-start) | async-done | bytes 4194336 | tf_op jit(solution)/shard_map/all_to_all | solution.py:62
  155.0 4.6 copy.52
  159.6 3.7 fusion.54
  163.3 8.1 copy.34
  171.3 5.3 all-to-all-start.1
  177.8 9.1 copy.37
  186.9 134.8 %all-to-all-done.1 = f32[16,2,256,256]{3,2,1,0:T(8,128)} async-done(((f32[16,2,256,256]{3,2,1,0:T(8,128)}), f32[16,2,256,256]{3,2,1,0:T(8,128)}, u32[]{:S(2)}, u32[]{:S(2)}) %all-to-all-start.1) | async-done | bytes 8388640 | tf_op jit(solution)/shard_map/all_to_all | solution.py:75
  321.7 17.3 %fusion.2 = f32[8,256,4,256]{3,0,1,2:T(8,128)} fusion(f32[32]{0:T(128)S(1)} %mul.78, s32[8,4]{0,1:T(4,128)S(1)} %multiply_add_fusion, s32[32]{0:T(128)S(1)} %add.154, f32[4,8,256,256]{3,2,1,0:T(8,128)} %bitcast.51), kind=kOutput, calls=%fused_computation.12 | convolution fusion | flops 805308416 | bytes 16777600 | tf_op jit(solution)/shard_map/dot_general | solution.py:17
  339.0 10.8 %copy.36 = f32[8,256,4,256]{1,0,3,2:T(8,128)} copy(f32[8,256,4,256]{3,0,1,2:T(8,128)} %fusion.2) | data formatting | bytes 16777216 | tf_op jit(solution)/shard_map/transpose | solution.py:92
  349.8 10.7 %copy.54 = f32[128,8,8,256]{3,1,2,0:T(8,128)} copy(f32[128,8,8,256]{3,2,1,0:T(8,128)} %bitcast.170) | data formatting | bytes 16777216
  360.5 11.9 %sub.79 = f32[2048,1024]{0,1:T(8,128)} subtract(f32[2048,1024]{0,1:T(8,128)} %copy.37, f32[2048,1024]{0,1:T(8,128)} %bitcast.169) | non-fusion elementwise | flops 2097152 | bytes 25165824 | tf_op jit(solution)/shard_map/sub | solution.py:95
  372.4 1.0 slice_select_fusion.3
  373.5 1.0 fusion.13
  374.5 11.7 %cholesky.130 = f32[128,128]{1,0:T(8,128)S(1)} custom-call(f32[128,128]{1,0:T(8,128)S(1)} %cholesky.194), custom_call_target="Cholesky" | custom-call | tf_op jit(solution)/shard_map/jit(cholesky)/cholesky | solution.py:105
  386.3 10.0 %custom-call.13 = f32[1,128,128]{1,2,0:T(8,128)S(1)} custom-call(f32[1,128,128]{2,1,0:T(8,128)S(1)} %get-tuple-element.90), custom_call_target="InvertDiagBlocksLowerTriangular" | custom-call | tf_op jit(solution)/shard_map/jit(cholesky)/cholesky | solution.py:105
  396.7 11.7 %cholesky.147 = f32[128,128]{1,0:T(8,128)S(1)} custom-call(f32[128,128]{1,0:T(8,128)S(1)} %convolution_subtract_fusion.5), custom_call_target="Cholesky" | custom-call | tf_op jit(solution)/shard_map/jit(cholesky)/cholesky | solution.py:105
  408.5 0.7 compare_reduce_fusion.2
  410.6 4.1 while.6
  410.6 0.7 fusion.85
  411.3 1.3 bitcast_dynamic-update-slice_fusion.4
  412.7 0.7 fusion.85
  413.3 1.3 bitcast_dynamic-update-slice_fusion.4
  414.7 19.7 %custom-call.14 = f32[2,128,128]{1,2,0:T(8,128)S(1)} custom-call(f32[2,128,128]{2,1,0:T(8,128)S(1)} %get-tuple-element.42), custom_call_target="InvertDiagBlocksLowerTriangular" | custom-call | tf_op jit(solution)/shard_map/triangular_solve/custom-call.0 | solution.py:106
  435.4 0.8 maximum_select_fusion
  436.3 63.0 %all-reduce.8.cloned.1.call-done = f32[2,256,256]{2,1,0:T(8,128)} async-done(((f32[2,256,256]{2,1,0:T(8,128)}), f32[2,256,256]{2,1,0:T(8,128)}) %all-reduce.8.cloned.1.call-update) | async-done | bytes 524304 | tf_op jit(solution)/shard_map/psum | solution.py:13
  499.3 5.1 convolution_select_fusion.1
  504.6 1.5 broadcast_select_fusion.3
  506.1 89.7 %all-reduce.10.cloned.1.call-done = f32[2048,256]{1,0:T(8,128)} async-done(((f32[2048,256]{1,0:T(8,128)}), f32[2048,256]{1,0:T(8,128)}) %all-reduce.10.cloned.1.call-update) | async-done | bytes 2097168 | tf_op jit(solution)/shard_map/psum | solution.py:13
  595.9 3.2 broadcast_select_fusion.2
  599.1 64.4 %all-reduce.12.cloned.1.call-done = f32[2048,256]{1,0:T(8,128)} async-done(((f32[2048,256]{1,0:T(8,128)}), f32[2048,256]{1,0:T(8,128)}) %all-reduce.12.cloned.1.call-update) | async-done | bytes 2097168 | tf_op jit(solution)/shard_map/psum | solution.py:13
  663.6 10.5 %convolution_subtract_fusion.1 = f32[2048,1024]{0,1:T(8,128)S(1)} fusion(f32[2048,1024]{0,1:T(8,128)} %sub.79, f32[2048,256]{1,0:T(8,128)S(1)} %copy-done.3, f32[2048,256]{1,0:T(8,128)} %all-reduce.12.cloned.1.call-done, s32[]{:T(128)S(6)} %select_n.189), kind=kOutput, calls=%fused_computation.10 | convolution fusion | flops 6444548096 | bytes 19922948 | tf_op jit(solution)/shard_map/dot_general | solution.py:23
  674.0 3.4 copy-done.2
  677.6 1.0 fusion.12
  678.6 11.7 %cholesky.164 = f32[128,128]{1,0:T(8,128)S(1)} custom-call(f32[128,128]{1,0:T(8,128)S(1)} %cholesky.197), custom_call_target="Cholesky" | custom-call | tf_op jit(solution)/shard_map/jit(cholesky)/cholesky | solution.py:105
  690.4 0.6 compare_reduce_fusion.1
  691.0 9.8 custom-call.15
  701.3 11.7 %cholesky.181 = f32[128,128]{1,0:T(8,128)S(1)} custom-call(f32[128,128]{1,0:T(8,128)S(1)} %convolution_subtract_fusion.4), custom_call_target="Cholesky" | custom-call | tf_op jit(solution)/shard_map/jit(cholesky)/cholesky | solution.py:105
  713.1 0.7 compare_reduce_fusion
  715.2 4.1 while.7
  715.2 0.6 fusion.86
  715.8 1.4 bitcast_dynamic-update-slice_fusion.5
  717.3 0.6 fusion.86
  717.9 1.4 bitcast_dynamic-update-slice_fusion.5
  719.3 19.9 %custom-call.16 = f32[2,128,128]{1,2,0:T(8,128)S(1)} custom-call(f32[2,128,128]{2,1,0:T(8,128)S(1)} %get-tuple-element.43), custom_call_target="InvertDiagBlocksLowerTriangular" | custom-call | tf_op jit(solution)/shard_map/triangular_solve/custom-call.0 | solution.py:106
  740.3 0.8 maximum_select_fusion.1
  741.2 60.2 %all-reduce.14.cloned.1.call-done = f32[2,256,256]{2,1,0:T(8,128)} async-done(((f32[2,256,256]{2,1,0:T(8,128)}), f32[2,256,256]{2,1,0:T(8,128)}) %all-reduce.14.cloned.1.call-update) | async-done | bytes 524304 | tf_op jit(solution)/shard_map/psum | solution.py:13
  801.5 5.1 convolution_select_fusion
  806.7 1.5 broadcast_select_fusion.1
  808.2 89.8 %all-reduce.16.cloned.1.call-done = f32[2048,256]{1,0:T(8,128)} async-done(((f32[2048,256]{1,0:T(8,128)}), f32[2048,256]{1,0:T(8,128)}) %all-reduce.16.cloned.1.call-update) | async-done | bytes 2097168 | tf_op jit(solution)/shard_map/psum | solution.py:13
  898.0 3.1 broadcast_select_fusion
  901.1 4.2 pad_maximum_fusion
  905.3 60.0 %all-reduce.18.cloned.1.call-done = f32[2048,256]{1,0:T(8,128)} async-done(((f32[2048,256]{1,0:T(8,128)}), f32[2048,256]{1,0:T(8,128)}) %all-reduce.18.cloned.1.call-update) | async-done | bytes 2097168 | tf_op jit(solution)/shard_map/psum | solution.py:13
  965.3 11.8 %convolution_subtract_fusion = f32[2048,1024]{0,1:T(8,128)} fusion(f32[2048,1024]{0,1:T(8,128)} %copy-done.2, f32[2048,256]{1,0:T(8,128)} %all-reduce.16.cloned.1.call-done, f32[2048,256]{1,0:T(8,128)} %all-reduce.18.cloned.1.call-done, s32[]{:T(128)S(6)} %select_n.189), kind=kOutput, calls=%fused_computation.9 | convolution fusion | flops 6444548096 | bytes 19922948 | tf_op jit(solution)/shard_map/dot_general | solution.py:23
  977.1 9.3 copy.44
  (84 shorter events, 5.7 us)
Async XLA Ops:
  7.2 1.2 copy-start
  7.2 77.6 %all-gather.2.cloned.1.call-start = ((), (), s32[]{:S(2)}) async-start(), calls=%async_computation.2 | async-start | bytes 8912896 | tf_op jit(solution)/shard_map/all_gather | solution.py:52
  100.4 4.9 copy-start.6
  100.4 54.5 %all-to-all-start = ((f32[8,2,256,256]{3,2,1,0:T(8,128)}), f32[8,2,256,256]{3,2,1,0:T(8,128)}, u32[]{:S(2)}, u32[]{:S(2)}) async-start(f32[8,2,256,256]{3,2,1,0:T(8,128)} %bitcast.172), calls=%async_computation | async-start | bytes 8388608 | tf_op jit(solution)/shard_map/all_to_all | solution.py:62
  171.3 150.4 %all-to-all-start.1 = ((f32[16,2,256,256]{3,2,1,0:T(8,128)}), f32[16,2,256,256]{3,2,1,0:T(8,128)}, u32[]{:S(2)}, u32[]{:S(2)}) async-start(f32[16,2,256,256]{3,2,1,0:T(8,128)} %copy.34), calls=%async_computation.1 | async-start | bytes 16777216 | tf_op jit(solution)/shard_map/all_to_all | solution.py:75
  176.7 322.7 %all-reduce.8.cloned.1.call-start = ((), (), s32[]{:S(2)}) async-start(), calls=%async_computation.3 | async-start | bytes 1048576 | tf_op jit(solution)/shard_map/psum | solution.py:13
  436.3 159.6 %all-reduce.10.cloned.1.call-start = ((), (), s32[]{:S(2)}) async-start(), calls=%async_computation.4 | async-start | bytes 4194304 | tf_op jit(solution)/shard_map/psum | solution.py:13
  499.3 5.2 copy-start.5
  506.0 157.5 %all-reduce.12.cloned.1.call-start = ((), (), s32[]{:S(2)}) async-start(), calls=%async_computation.5 | async-start | bytes 4194304 | tf_op jit(solution)/shard_map/psum | solution.py:13
  595.8 67.7 %copy-start.3 = (f32[2048,256]{1,0:T(8,128)S(1)}, f32[2048,256]{1,0:T(8,128)}, u32[]{:S(2)}) copy-start(f32[2048,256]{1,0:T(8,128)} %all-reduce.10.cloned.1.call-done) | copy-start | bytes 6291460
  599.1 202.4 %all-reduce.14.cloned.1.call-start = ((), (), s32[]{:S(2)}) async-start(), calls=%async_computation.6 | async-start | bytes 1048576 | tf_op jit(solution)/shard_map/psum | solution.py:13
  674.0 3.4 copy-start.2
  741.2 156.8 %all-reduce.16.cloned.1.call-start = ((), (), s32[]{:S(2)}) async-start(), calls=%async_computation.7 | async-start | bytes 4194304 | tf_op jit(solution)/shard_map/psum | solution.py:13
  801.5 5.2 copy-start.4
  808.2 157.1 %all-reduce.18.cloned.1.call-start = ((), (), s32[]{:S(2)}) async-start(), calls=%async_computation.8 | async-start | bytes 4194304 | tf_op jit(solution)/shard_map/psum | solution.py:13
  977.1 9.3 copy-start.1
Sparse Core Ops, SparseCore 0:
  11.4 73.3 all-gather.1
  436.4 62.9 all-reduce.7
  506.2 89.6 all-reduce.9
  599.2 64.3 all-reduce.11
  741.3 60.1 all-reduce.13
  808.3 89.6 all-reduce.15
  901.2 64.0 all-reduce.17
where the time goes:
time: 999 us; the launch traced here: 994 us
  waiting for transfers between devices  682 us (68%)
  other arithmetic  141 us (14%)
  local copies, waits for them, and re-layouts  71.9 us (7%)
  matrix products  70 us (7%)
  between operations  17.6 us (2%)
  starting transfers between devices  10.7 us (1%)
    psum x6, waiting for transfers between devices, from_root(): return lax.psum(block, axis)  427 us
    all_to_all x1, waiting for transfers between devices, per_device(): lax.all_to_all(outgoing_cols, 'col', split_axis=0, concat_axis=0, tiled=T...  135 us
    all_gather x1, waiting for transfers between devices, per_device(): lax.all_gather(own_factor, 'col', axis=0, tiled=True)  70.5 us
    another operation x13, other arithmetic, per_device(): pivot_tile = jnp.linalg.cholesky(diag_tile)  68.8 us
    all_to_all x1, waiting for transfers between devices, per_device(): lax.all_to_all(outgoing, 'row', split_axis=0, concat_axis=0, tiled=True)  49.4 us
    dot_general x6, matrix products, product_rows(): lax.dot_general(matrix_a, matrix_b, (((1,), (1,)), ((), ())), precision=l...  46 us
    another operation x3, other arithmetic, per_device(): lax.linalg.triangular_solve(pivot_tile, identity, left_side=True, lower=T...  39.6 us
    unnamed x18, local copies, waits for them, and re-layouts  38.4 us
  transfers between devices with their start and end apart: 9, of which 9 were waited for; matrix products, arithmetic and copies ran while one was open for 2% of the time, Pallas kernels for 0%

commit v1 on v0

--- a/solution.py
+++ b/solution.py
@@ -6,6 +6,11 @@
 TILE = 256
 PCT = 4
 NSP = 2
+
+
+def all_by_exchange(value, mesh_axis, d):
+    sent = jnp.stack([value] * lax.axis_size(mesh_axis))
+    return jnp.concatenate(lax.all_to_all(sent, mesh_axis, 0, 0), axis=d)
 
 
 def from_root(block, axis, holder):
@@ -49,7 +54,7 @@
     own_factor = product_rows(child_panels[0], child_inverses[0])
     my_list = lax.dynamic_index_in_dim(parent_index, here_row, 0, keepdims=False)
     block_of = parent_index // PCT
-    update_col = product_rows(lax.all_gather(own_factor, "col", axis=0, tiled=True), own_factor)
+    update_col = product_rows(all_by_exchange(own_factor, "col", 0), own_factor)
     dest_row = my_list // PCT // per_block
     tile_ids = jnp.arange(col_devices, dtype=jnp.int32)
     same_dest = (dest_row[None, :] == dest_row[:, None]) & (tile_ids[None, :] < tile_ids[:, None])

time: 999 us -> 1090 us (1.091)
  waiting for transfers between devices: 682 us -> 758 us
  starting transfers between devices: 10.7 us -> 21.9 us
    all_to_all x0 -> x1, waiting for transfers between devices: none -> 147 us  [all_by_exchange(): return jnp.concatenate(lax.all_to_all(sent, mesh_axis, 0, 0), axis=d)]
    all_gather x1 -> x0, waiting for transfers between devices: 70.5 us -> none  [per_device(): lax.all_gather(own_factor, 'col', axis=0, tiled=True)]
  transfers between devices with their start and end apart: 9 -> 9, of which waited for: 9 -> 9; matrix products, arithmetic and copies ran while one was open for 2% -> 1% of each run, Pallas kernels for 0% -> 0%
where the time goes in v1:
time: 1090 us; the launch traced here: 1080 us
  waiting for transfers between devices  758 us (70%)
  other arithmetic  139 us (13%)
  local copies, waits for them, and re-layouts  76.4 us (7%)
  matrix products  69.1 us (6%)
  starting transfers between devices  21.9 us (2%)
  between operations  17.6 us (2%)
    psum x6, waiting for transfers between devices, from_root(): return lax.psum(block, axis)  427 us
    all_to_all x1, waiting for transfers between devices, all_by_exchange(): return jnp.concatenate(lax.all_to_all(sent, mesh_axis, 0, 0), axis=d)  147 us
    all_to_all x1, waiting for transfers between devices, per_device(): lax.all_to_all(outgoing_cols, 'col', split_axis=0, concat_axis=0, tiled=T...  135 us
    another operation x13, other arithmetic, per_device(): pivot_tile = jnp.linalg.cholesky(diag_tile)  68.8 us
    all_to_all x1, waiting for transfers between devices, per_device(): lax.all_to_all(outgoing, 'row', split_axis=0, concat_axis=0, tiled=True)  49.4 us
    dot_general x6, matrix products, product_rows(): lax.dot_general(matrix_a, matrix_b, (((1,), (1,)), ((), ())), precision=l...  45.1 us
    another operation x3, other arithmetic, per_device(): lax.linalg.triangular_solve(pivot_tile, identity, left_side=True, lower=T...  39.6 us
    unnamed x18, local copies, waits for them, and re-layouts  38.4 us
  transfers between devices with their start and end apart: 9, of which 9 were waited for; matrix products, arithmetic and copies ran while one was open for 1% of the time, Pallas kernels for 0%

profile of v1, /device:TPU:0, one launch (start us, length us, event | category | flops | bytes accessed | tf_op | source)
XLA Modules:
  0.0 1082.7 jit_solution(16493624821512441058)
XLA Ops:
  7.2 1.2 copy-done
  8.4 2.1 fusion.5
  10.5 4.5 stack.14
  15.0 8.3 all-to-all-start
  23.6 0.6 scatter_custom_fusion
  24.2 146.7 %all-to-all-done = f32[16,256,512]{2,1,0:T(8,128)} async-done(((f32[16,256,512]{2,1,0:T(8,128)}), f32[16,256,512]{2,1,0:T(8,128)}, u32[]{:S(2)}, u32[]{:S(2)}) %all-to-all-start) | async-done | bytes 8388640 | tf_op jit(solution)/shard_map/all_to_all | solution.py:13
  171.0 10.5 fusion.9
  181.5 5.0 gather_fusion
  186.5 4.7 all-to-all-start.1
  191.4 49.4 %all-to-all-done.1 = f32[8,2,256,256]{3,2,1,0:T(8,128)} async-done(((f32[8,2,256,256]{3,2,1,0:T(8,128)}), f32[8,2,256,256]{3,2,1,0:T(8,128)}, u32[]{:S(2)}, u32[]{:S(2)}) %all-to-all-start.1) | async-done | bytes 4194336 | tf_op jit(solution)/shard_map/all_to_all | solution.py:67
  240.9 4.6 copy.52
  245.5 3.7 fusion.56
  249.2 8.1 copy.34
  257.3 8.4 all-to-all-start.2
  266.7 9.1 copy.37
  275.9 134.8 %all-to-all-done.2 = f32[16,2,256,256]{3,2,1,0:T(8,128)} async-done(((f32[16,2,256,256]{3,2,1,0:T(8,128)}), f32[16,2,256,256]{3,2,1,0:T(8,128)}, u32[]{:S(2)}, u32[]{:S(2)}) %all-to-all-start.2) | async-done | bytes 8388640 | tf_op jit(solution)/shard_map/all_to_all | solution.py:80
  410.7 17.3 %fusion.2 = f32[8,256,4,256]{3,0,1,2:T(8,128)} fusion(f32[32]{0:T(128)S(1)} %mul.78, s32[8,4]{0,1:T(4,128)S(1)} %multiply_add_fusion, s32[32]{0:T(128)S(1)} %add.154, f32[4,8,256,256]{3,2,1,0:T(8,128)} %bitcast.51), kind=kOutput, calls=%fused_computation.12 | convolution fusion | flops 805308416 | bytes 16777600 | tf_op jit(solution)/shard_map/dot_general | solution.py:22
  428.0 10.8 copy.36
  438.8 10.7 copy.54
  449.5 11.9 %sub.79 = f32[2048,1024]{0,1:T(8,128)} subtract(f32[2048,1024]{0,1:T(8,128)} %copy.37, f32[2048,1024]{0,1:T(8,128)} %bitcast.170) | non-fusion elementwise | flops 2097152 | bytes 25165824 | tf_op jit(solution)/shard_map/sub | solution.py:100
  461.3 1.0 slice_select_fusion.3
  462.5 1.0 fusion.15
  463.5 11.7 %cholesky.130 = f32[128,128]{1,0:T(8,128)S(1)} custom-call(f32[128,128]{1,0:T(8,128)S(1)} %cholesky.194), custom_call_target="Cholesky" | custom-call | tf_op jit(solution)/shard_map/jit(cholesky)/cholesky | solution.py:110
  475.2 10.0 custom-call.13
  485.7 11.7 %cholesky.147 = f32[128,128]{1,0:T(8,128)S(1)} custom-call(f32[128,128]{1,0:T(8,128)S(1)} %convolution_subtract_fusion.5), custom_call_target="Cholesky" | custom-call | tf_op jit(solution)/shard_map/jit(cholesky)/cholesky | solution.py:110
  497.4 0.7 compare_reduce_fusion.2
  499.5 4.1 while.6
  499.6 0.7 fusion.85
  500.2 1.3 bitcast_dynamic-update-slice_fusion.4
  501.6 0.7 fusion.85
  502.3 1.3 bitcast_dynamic-update-slice_fusion.4
  503.6 19.7 %custom-call.14 = f32[2,128,128]{1,2,0:T(8,128)S(1)} custom-call(f32[2,128,128]{2,1,0:T(8,128)S(1)} %get-tuple-element.42), custom_call_target="InvertDiagBlocksLowerTriangular" | custom-call | tf_op jit(solution)/shard_map/triangular_solve/custom-call.0 | solution.py:111
  524.4 0.8 maximum_select_fusion
  525.3 63.0 %all-reduce.8.cloned.1.call-done = f32[2,256,256]{2,1,0:T(8,128)} async-done(((f32[2,256,256]{2,1,0:T(8,128)}), f32[2,256,256]{2,1,0:T(8,128)}) %all-reduce.8.cloned.1.call-update) | async-done | bytes 524304 | tf_op jit(solution)/shard_map/psum | solution.py:18
  588.3 5.1 convolution_select_fusion.1
  593.5 1.5 broadcast_select_fusion.3
  595.1 89.7 %all-reduce.10.cloned.1.call-done = f32[2048,256]{1,0:T(8,128)} async-done(((f32[2048,256]{1,0:T(8,128)}), f32[2048,256]{1,0:T(8,128)}) %all-reduce.10.cloned.1.call-update) | async-done | bytes 2097168 | tf_op jit(solution)/shard_map/psum | solution.py:18
  684.8 3.2 broadcast_select_fusion.2
  688.1 64.6 %all-reduce.12.cloned.1.call-done = f32[2048,256]{1,0:T(8,128)} async-done(((f32[2048,256]{1,0:T(8,128)}), f32[2048,256]{1,0:T(8,128)}) %all-reduce.12.cloned.1.call-update) | async-done | bytes 2097168 | tf_op jit(solution)/shard_map/psum | solution.py:18
  752.7 10.5 convolution_subtract_fusion.1
  763.1 3.4 copy-done.2
  766.7 1.0 fusion.14
  767.7 11.7 %cholesky.164 = f32[128,128]{1,0:T(8,128)S(1)} custom-call(f32[128,128]{1,0:T(8,128)S(1)} %cholesky.197), custom_call_target="Cholesky" | custom-call | tf_op jit(solution)/shard_map/jit(cholesky)/cholesky | solution.py:110
  779.5 0.6 compare_reduce_fusion.1
  780.1 9.8 custom-call.15
  790.4 11.7 %cholesky.181 = f32[128,128]{1,0:T(8,128)S(1)} custom-call(f32[128,128]{1,0:T(8,128)S(1)} %convolution_subtract_fusion.4), custom_call_target="Cholesky" | custom-call | tf_op jit(solution)/shard_map/jit(cholesky)/cholesky | solution.py:110
  802.2 0.7 compare_reduce_fusion
  804.3 4.1 while.7
  804.3 0.6 fusion.86
  804.9 1.4 bitcast_dynamic-update-slice_fusion.5
  806.4 0.6 fusion.86
  807.0 1.4 bitcast_dynamic-update-slice_fusion.5
  808.4 19.9 %custom-call.16 = f32[2,128,128]{1,2,0:T(8,128)S(1)} custom-call(f32[2,128,128]{2,1,0:T(8,128)S(1)} %get-tuple-element.43), custom_call_target="InvertDiagBlocksLowerTriangular" | custom-call | tf_op jit(solution)/shard_map/triangular_solve/custom-call.0 | solution.py:111
  828.7 0.4 convolution_subtract_fusion.2
  829.4 0.8 maximum_select_fusion.1
  830.3 60.3 %all-reduce.14.cloned.1.call-done = f32[2,256,256]{2,1,0:T(8,128)} async-done(((f32[2,256,256]{2,1,0:T(8,128)}), f32[2,256,256]{2,1,0:T(8,128)}) %all-reduce.14.cloned.1.call-update) | async-done | bytes 524304 | tf_op jit(solution)/shard_map/psum | solution.py:18
  890.6 5.1 convolution_select_fusion
  895.8 1.5 broadcast_select_fusion.1
  897.3 89.8 %all-reduce.16.cloned.1.call-done = f32[2048,256]{1,0:T(8,128)} async-done(((f32[2048,256]{1,0:T(8,128)}), f32[2048,256]{1,0:T(8,128)}) %all-reduce.16.cloned.1.call-update) | async-done | bytes 2097168 | tf_op jit(solution)/shard_map/psum | solution.py:18
  987.1 3.1 broadcast_select_fusion
  990.2 4.2 pad_maximum_fusion
  994.4 59.9 %all-reduce.18.cloned.1.call-done = f32[2048,256]{1,0:T(8,128)} async-done(((f32[2048,256]{1,0:T(8,128)}), f32[2048,256]{1,0:T(8,128)}) %all-reduce.18.cloned.1.call-update) | async-done | bytes 2097168 | tf_op jit(solution)/shard_map/psum | solution.py:18
  1054.2 11.8 %convolution_subtract_fusion = f32[2048,1024]{0,1:T(8,128)} fusion(f32[2048,1024]{0,1:T(8,128)} %copy-done.2, f32[2048,256]{1,0:T(8,128)} %all-reduce.16.cloned.1.call-done, f32[2048,256]{1,0:T(8,128)} %all-reduce.18.cloned.1.call-done, s32[]{:T(128)S(6)} %select_n.189), kind=kOutput, calls=%fused_computation.9 | convolution fusion | flops 6444548096 | bytes 19922948 | tf_op jit(solution)/shard_map/dot_general | solution.py:28
  1066.0 9.3 copy.44
  (84 shorter events, 5.3 us)
Async XLA Ops:
  7.2 1.2 copy-start
  15.0 8.3 copy-start.6
  15.0 156.0 %all-to-all-start = ((f32[16,256,512]{2,1,0:T(8,128)}), f32[16,256,512]{2,1,0:T(8,128)}, u32[]{:S(2)}, u32[]{:S(2)}) async-start(f32[16,256,512]{2,1,0:T(8,128)} %stack.14), calls=%async_computation | async-start | bytes 16777216 | tf_op jit(solution)/shard_map/all_to_all | solution.py:13
  186.5 54.4 %all-to-all-start.1 = ((f32[8,2,256,256]{3,2,1,0:T(8,128)}), f32[8,2,256,256]{3,2,1,0:T(8,128)}, u32[]{:S(2)}, u32[]{:S(2)}) async-start(f32[8,2,256,256]{3,2,1,0:T(8,128)} %bitcast.172), calls=%async_computation.1 | async-start | bytes 8388608 | tf_op jit(solution)/shard_map/all_to_all | solution.py:67
  257.3 153.4 %all-to-all-start.2 = ((f32[16,2,256,256]{3,2,1,0:T(8,128)}), f32[16,2,256,256]{3,2,1,0:T(8,128)}, u32[]{:S(2)}, u32[]{:S(2)}) async-start(f32[16,2,256,256]{3,2,1,0:T(8,128)} %copy.34), calls=%async_computation.2 | async-start | bytes 16777216 | tf_op jit(solution)/shard_map/all_to_all | solution.py:80
  265.6 322.7 %all-reduce.8.cloned.1.call-start = ((), (), s32[]{:S(2)}) async-start(), calls=%async_computation.3 | async-start | bytes 1048576 | tf_op jit(solution)/shard_map/psum | solution.py:18
  525.2 159.6 %all-reduce.10.cloned.1.call-start = ((), (), s32[]{:S(2)}) async-start(), calls=%async_computation.4 | async-start | bytes 4194304 | tf_op jit(solution)/shard_map/psum | solution.py:18
  588.3 5.2 copy-start.5
  595.0 157.7 %all-reduce.12.cloned.1.call-start = ((), (), s32[]{:S(2)}) async-start(), calls=%async_computation.5 | async-start | bytes 4194304 | tf_op jit(solution)/shard_map/psum | solution.py:18
  684.8 67.9 %copy-start.3 = (f32[2048,256]{1,0:T(8,128)S(1)}, f32[2048,256]{1,0:T(8,128)}, u32[]{:S(2)}) copy-start(f32[2048,256]{1,0:T(8,128)} %all-reduce.10.cloned.1.call-done) | copy-start | bytes 6291460
  688.0 202.6 %all-reduce.14.cloned.1.call-start = ((), (), s32[]{:S(2)}) async-start(), calls=%async_computation.6 | async-start | bytes 1048576 | tf_op jit(solution)/shard_map/psum | solution.py:18
  763.1 3.4 copy-start.2
  830.3 156.8 %all-reduce.16.cloned.1.call-start = ((), (), s32[]{:S(2)}) async-start(), calls=%async_computation.7 | async-start | bytes 4194304 | tf_op jit(solution)/shard_map/psum | solution.py:18
  890.6 5.2 copy-start.4
  897.3 156.9 %all-reduce.18.cloned.1.call-start = ((), (), s32[]{:S(2)}) async-start(), calls=%async_computation.8 | async-start | bytes 4194304 | tf_op jit(solution)/shard_map/psum | solution.py:18
  1066.0 9.3 copy-start.1
Sparse Core Ops, SparseCore 0:
  525.3 62.9 all-reduce.7
  595.1 89.6 all-reduce.9
  688.1 64.4 all-reduce.11
  830.4 60.1 all-reduce.13
  897.4 89.6 all-reduce.15
  990.3 63.8 all-reduce.17
